TPU v7x, 32 devices: a whole 2x2x4 slice. The times are simulated.
32 devices in a mesh: heads: 4 (over y, core), seq: 8 (over z, x).
Axes of the slice: x: 2, y: 2, z: 4, core: 2. Of those that a mesh axis runs over, the one named last changes fastest.
Arguments:
- queries: bfloat16 [1024, 64, 576], P('seq', 'heads'), may hold values from -6 to 6
- latents: bfloat16 [8, 128, 576], P('seq', 'heads'), may hold values from -6 to 6
- grad_out: bfloat16 [1024, 64, 512], P('seq', 'heads'), may hold values from -6 to 6
- selected: int32 [8, 4], P('seq'), may hold values from 0 to 7, as said below
Outputs:
- output: bfloat16 [1024, 64, 512], P('seq', 'heads')
- grad_query: bfloat16 [1024, 64, 576], P('seq', 'heads')
- latent_grad: float32 [8, 128, 576], P('seq', 'heads')
Inputs may be any that keep to these rules, and one draw needn't show every extreme that they name: `selected`: row i lists 4 different blocks, none of them held on the same index of seq as block i (blocks i and j share it when i // 1 equals j // 1); how often a block is chosen varies widely between blocks.
All inputs are finite; a program needn't handle non-finite values.
Results may differ from a plain program's by a relative error of at most 0.012.
Values may be sent and summed in bfloat16 or wider, within the bound.
A program may use at most 64 MiB of HBM per device.

v0:
```python
import jax
import jax.numpy as jnp
from jax import lax
from jax.sharding import PartitionSpec as P


def shards(queries, latents, grad_out, selected):
    block_count, row_share, key_width = latents.shape
    token_total, head_count, _ = queries.shape
    value_width = grad_out.shape[2]
    key_blocks = selected.shape[1] + 1
    block_size = token_total // block_count
    score_scale = key_width ** (-0.5)
    slices = lax.all_gather(latents, "seq", axis=0, tiled=True)
    list_blocks = slices.shape[0]
    own_blocks = lax.axis_index("seq") * block_count + jnp.arange(block_count, dtype=jnp.int32)
    block_ids = jnp.concatenate([own_blocks[:, None], selected], axis=1).reshape(-1)
    picked = jnp.take(slices, block_ids, axis=0)
    key_row_tiles = lax.all_gather(picked, "heads", axis=1, tiled=True)
    key_row_tiles = key_row_tiles.reshape(block_count, key_blocks * block_size, key_width)
    value_rows = key_row_tiles[:, :, :value_width]
    query_row_tiles = queries.reshape(block_count, block_size, head_count, key_width)
    grad_rows = grad_out.reshape(block_count, block_size, head_count, value_width)
    scores = (
        jnp.einsum(
            "gonv,gmv->gnom", query_row_tiles, key_row_tiles, preferred_element_type=jnp.float32
        )
        * score_scale
    )
    prob_full = jax.nn.softmax(scores, axis=-1)
    prob_half = prob_full.astype(jnp.bfloat16)
    output = jnp.einsum(
        "bhtk,bkl->bthl", prob_half, value_rows, preferred_element_type=jnp.float32
    ).astype(jnp.bfloat16)
    row_delta = jnp.sum(grad_rows.astype(jnp.float32) * output.astype(jnp.float32), axis=-1)
    grad_prob = jnp.einsum(
        "bthl,bkl->bhtk", grad_rows, value_rows, preferred_element_type=jnp.float32
    )
    score_gradient = (
        prob_full * (grad_prob - jnp.transpose(row_delta, (0, 2, 1))[..., None]) * score_scale
    ).astype(jnp.bfloat16)
    grad_query = jnp.einsum(
        "mfgv,mvq->mgfq", score_gradient, key_row_tiles, preferred_element_type=jnp.float32
    ).astype(jnp.bfloat16)
    key_gradient = jnp.einsum(
        "jxnq,jnxa->jqa", score_gradient, query_row_tiles, preferred_element_type=jnp.float32
    )
    grad_value = jnp.einsum(
        "bhtk,bthl->bkl", prob_half, grad_rows, preferred_element_type=jnp.float32
    )
    key_gradient = jnp.concatenate(
        [key_gradient[:, :, :value_width] + grad_value, key_gradient[:, :, value_width:]], axis=-1
    )
    contrib = key_gradient.reshape(block_count * key_blocks, block_size, key_width)
    head_total = lax.psum(contrib, "heads")
    own_share = lax.dynamic_slice_in_dim(
        head_total, lax.axis_index("heads") * row_share, row_share, 1
    )
    one_hot = (jnp.arange(list_blocks, dtype=jnp.int32)[:, None] == block_ids[None, :]).astype(
        jnp.float32
    )
    dense_grad = jnp.dot(
        one_hot,
        own_share.reshape(block_count * key_blocks, row_share * key_width),
        precision=lax.Precision.HIGHEST,
        preferred_element_type=jnp.float32,
    )
    dense_grad = dense_grad.reshape(list_blocks, row_share, key_width)
    holders = list_blocks // block_count
    bundles = dense_grad.reshape(1, holders * block_count, row_share, key_width)
    arrived = lax.all_to_all(bundles, "seq", split_axis=1, concat_axis=0, tiled=True)
    latent_grad = jnp.sum(arrived, axis=0)
    return (
        output.reshape(token_total, head_count, value_width),
        grad_query.reshape(token_total, head_count, key_width),
        latent_grad,
    )


def solution(mesh):
    in_specs = (
        P("seq", "heads", None),
        P("seq", "heads", None),
        P("seq", "heads", None),
        P("seq", None),
    )
    out_specs = (P("seq", "heads", None), P("seq", "heads", None), P("seq", "heads", None))
    return jax.shard_map(shards, mesh=mesh, in_specs=in_specs, out_specs=out_specs, check_vma=False)
```

profile of v0, /device:TPU:0, one launch (start us, length us, event | category | flops | bytes accessed | tf_op | source)
XLA Modules:
  0.0 150.2 jit_solution(12962128840217296627)
XLA Ops:
  7.2 0.0 copy-start
  7.2 0.0 all-reduce.2.cloned.1.call-start
  7.2 0.9 compare_and_fusion
  8.1 32.9 %all_gather.6 = bf16[8,32,576]{2,1,0:T(8,128)(2,1)S(1)} all-gather(bf16[1,32,576]{2,1,0:T(8,128)(2,1)} %param.5), channel_id=1, replica_groups=mesh['heads'=4,'seq'=8] {'seq'}, dimensions={0}, use_global_device_ids=true | all-gather | bytes 331776 | tf_op jit(solution)/shard_map/all_gather | solution.py:14
  41.0 0.6 gather_fusion
  41.6 0.1 broadcast_select_fusion
  41.7 8.8 %all_gather.7 = bf16[5,128,576]{2,1,0:T(8,128)(2,1)S(1)} all-gather(bf16[5,32,576]{2,1,0:T(8,128)(2,1)S(1)} %broadcast_select_fusion), channel_id=1, replica_groups=mesh['heads'=4,'seq'=8] {'heads'}, dimensions={1}, use_global_device_ids=true | all-gather | bytes 921600 | tf_op jit(solution)/shard_map/all_gather | solution.py:19
  50.5 4.8 %copy.37 = bf16[128,16,512]{0,2,1:T(8,128)(2,1)} copy(bf16[128,16,512]{2,1,0:T(8,128)(2,1)} %param.6) | data formatting | bytes 4194304 | tf_op args[2]
  55.3 0.0 copy-done
  55.3 2.2 %bitcast_reduce_fusion = (f32[16,128]{1,0:T(8,128)S(1)}, f32[640,128,16]{1,0,2:T(8,128)S(1)}) fusion(bf16[640,576,1]{1,0,2:T(8,128)(2,1)S(1)} %bitcast.124, bf16[128,16,576]{0,2,1:T(8,128)(2,1)S(1)} %copy-done), kind=kOutput, calls=%fused_computation.6 | convolution fusion | flops 1512568832 | bytes 8347648 | tf_op jit(solution)/shard_map/gonv,gmv->gnom/dot_general | solution.py:25
  57.5 0.0 copy-start.1
  57.5 0.9 fusion.5
  58.4 0.7 copy-done.1
  59.1 3.5 %fusion.6 = (f32[128,16]{0,1:T(8,128)S(1)}, bf16[512,16,128]{2,0,1:T(8,128)(2,1)}) fusion(bf16[128,16,512]{0,2,1:T(8,128)(2,1)S(1)} %copy-done.1, f32[16,128]{1,0:T(8,128)S(1)} %fusion.5, f32[16,128]{1,0:T(8,128)S(1)} %get-tuple-element.14, f32[640,128,16]{1,0,2:T(8,128)S(1)} %get-tuple-element.15, bf16[1,640,576]{2,1,0:T(8,128)(2,1)S(1)} %bitcast.125), kind=kOutput, calls=%fused_computation.11 | convolution fusion | flops 1352660992 | bytes 10117120 | tf_op jit(solution)/shard_map/bhtk,bkl->bthl/dot_general | solution.py:32
  62.6 2.0 %fusion.7 = bf16[16,128,640]{1,2,0:T(8,128)(2,1)S(1)} fusion(f32[16,128]{1,0:T(8,128)S(1)} %bitcast.130, f32[16,128]{1,0:T(8,128)S(1)} %fusion.5, f32[16,128]{1,0:T(8,128)S(1)} %get-tuple-element.14, f32[640,128,16]{1,0,2:T(8,128)S(1)} %get-tuple-element.15, bf16[128,16,512]{0,2,1:T(8,128)(2,1)S(1)} %copy-done.1, bf16[1,640,576]{2,1,0:T(8,128)(2,1)S(1)} %bitcast.126), kind=kOutput, calls=%fused_computation.12 | convolution fusion | flops 1351352320 | bytes 10641408 | tf_op jit(solution)/shard_map/bthl,bkl->bhtk/dot_general | solution.py:36
  64.6 2.0 %convolution_bitcast_fusion = f32[1,640,576]{1,2,0:T(8,128)S(1)} fusion(bf16[16,128,640]{1,2,0:T(8,128)(2,1)S(1)} %fusion.7, bf16[128,16,576]{0,2,1:T(8,128)(2,1)S(1)} %copy-done), kind=kOutput, calls=%fused_computation.21 | convolution fusion | flops 1509949440 | bytes 6455296 | tf_op jit(solution)/shard_map/jxnq,jnxa->jqa/dot_general | solution.py:45
  66.6 0.0 copy-done.3
  66.6 1.9 %fusion.19 = f32[1,640,512]{1,2,0:T(8,128)S(1)} fusion(bf16[128,16,512]{0,2,1:T(8,128)(2,1)S(1)} %copy-done.1, f32[1,640,576]{1,2,0:T(8,128)S(1)} %convolution_bitcast_fusion, f32[16,128]{1,0:T(8,128)S(1)} %fusion.5, f32[16,128]{1,0:T(8,128)S(1)} %get-tuple-element.14, f32[640,128,16]{1,0,2:T(8,128)S(1)} %get-tuple-element.15), kind=kOutput, calls=%fused_computation.23 | convolution fusion | flops 1347747840 | bytes 9977856 | tf_op jit(solution)/shard_map/bhtk,bthl->bkl/dot_general | solution.py:48
  68.6 1.2 pad_maximum_fusion
  69.8 3.0 %copy.43 = f32[1,640,576]{2,1,0:T(8,128)} copy(f32[1,640,576]{1,2,0:T(8,128)} %pad_maximum_fusion) | data formatting | bytes 2949120 | tf_op jit(solution)/shard_map/concatenate | solution.py:51
  72.8 0.0 all-reduce.2.cloned.1.call-update
  72.8 44.1 %all-reduce.2.cloned.1.call-done = f32[5,128,576]{2,1,0:T(8,128)} async-done(((f32[5,128,576]{2,1,0:T(8,128)}), f32[5,128,576]{2,1,0:T(8,128)}) %all-reduce.2.cloned.1.call-update) | async-done | bytes 1474576 | tf_op jit(solution)/shard_map/psum | solution.py:55
  117.0 1.0 constant_dynamic-slice_fusion
  118.0 0.2 reshape.186
  118.2 0.2 dot_general.43
  118.4 0.7 convolution_bitcast_fusion.1
  119.1 1.0 copy.45
  120.0 5.5 %all-to-all-start = ((f32[1,8,32,576]{3,2,0,1:T(8,128)}), f32[1,8,32,576]{3,2,0,1:T(8,128)S(1)}, u32[]{:S(2)}, u32[]{:S(2)}) async-start(f32[1,8,32,576]{3,2,0,1:T(8,128)} %copy.45), calls=%async_computation | async-start | bytes 1310720 | tf_op jit(solution)/shard_map/all_to_all | solution.py:71
  125.5 4.5 %copy.46 = bf16[128,16,512]{2,1,0:T(8,128)(2,1)} copy(bf16[128,16,512]{0,2,1:T(8,128)(2,1)} %bitcast.123) | data formatting | bytes 4194304
  130.1 5.4 %convert_bitcast_fusion = bf16[128,16,576]{0,2,1:T(8,128)(2,1)} fusion(bf16[640,576,1]{1,0,2:T(8,128)(2,1)} %bitcast.127, bf16[16,128,640]{1,2,0:T(8,128)(2,1)} %copy-done.3), kind=kOutput, calls=%fused_computation.18 | convolution fusion | flops 1511129088 | bytes 5718016 | tf_op jit(solution)/shard_map/mfgv,mvq->mgfq/dot_general | solution.py:42
  135.5 7.2 %all-to-all-done = f32[1,8,32,576]{3,2,0,1:T(8,128)S(1)} async-done(((f32[1,8,32,576]{3,2,0,1:T(8,128)}), f32[1,8,32,576]{3,2,0,1:T(8,128)S(1)}, u32[]{:S(2)}, u32[]{:S(2)}) %all-to-all-start) | async-done | bytes 589856 | tf_op jit(solution)/shard_map/all_to_all | solution.py:71
  142.7 0.7 reduce_sum.34
  (6 shorter events, 0.0 us)
Async XLA Ops:
  7.2 48.1 %copy-start = (bf16[128,16,576]{0,2,1:T(8,128)(2,1)S(1)}, bf16[128,16,576]{0,2,1:T(8,128)(2,1)}, u32[]{:S(2)}) copy-start(bf16[128,16,576]{0,2,1:T(8,128)(2,1)} %param.4) | copy-start | bytes 7077892
  7.2 109.8 %all-reduce.2.cloned.1.call-start = ((), (), s32[]{:S(2)}) async-start(), calls=%async_computation.1 | async-start | bytes 3276800 | tf_op jit(solution)/shard_map/psum | solution.py:55
  50.5 12.1 %copy-start.2 = (bf16[5,128,576]{2,1,0:T(8,128)(2,1)}, bf16[5,128,576]{2,1,0:T(8,128)(2,1)S(1)}, u32[]{:S(2)}) copy-start(bf16[5,128,576]{2,1,0:T(8,128)(2,1)S(1)} %all_gather.7) | copy-start | bytes 2211844
  57.5 1.6 %copy-start.1 = (bf16[128,16,512]{0,2,1:T(8,128)(2,1)S(1)}, bf16[128,16,512]{0,2,1:T(8,128)(2,1)}, u32[]{:S(2)}) copy-start(bf16[128,16,512]{0,2,1:T(8,128)(2,1)} %copy.37) | copy-start | bytes 6291460
  64.6 2.0 %copy-start.3 = (bf16[16,128,640]{1,2,0:T(8,128)(2,1)}, bf16[16,128,640]{1,2,0:T(8,128)(2,1)S(1)}, u32[]{:S(2)}) copy-start(bf16[16,128,640]{1,2,0:T(8,128)(2,1)S(1)} %fusion.7) | copy-start | bytes 7864324
  120.0 22.7 %all-to-all-start = ((f32[1,8,32,576]{3,2,0,1:T(8,128)}), f32[1,8,32,576]{3,2,0,1:T(8,128)S(1)}, u32[]{:S(2)}, u32[]{:S(2)}) async-start(f32[1,8,32,576]{3,2,0,1:T(8,128)} %copy.45), calls=%async_computation | async-start | bytes 1310720 | tf_op jit(solution)/shard_map/all_to_all | solution.py:71
Sparse Core Ops, SparseCore 0:
  73.0 43.9 all-reduce.1
where the time goes:
time: 151 us; the launch traced here: 150 us
  waiting for transfers between devices  51.3 us (34%)
  blocking collectives  41.7 us (28%)
  matrix products  17.7 us (12%)
  local copies, waits for them, and re-layouts  16.1 us (11%)
  between operations  14.1 us (9%)
  starting transfers between devices  5.55 us (4%)
  other arithmetic  3.74 us (2%)
    psum x1, waiting for transfers between devices, shards(): head_total = lax.psum(contrib, 'heads')  44.1 us
    all_gather x1, blocking collectives, shards(): slices = lax.all_gather(latents, 'seq', axis=0, tiled=True)  32.9 us
    unnamed x10, local copies, waits for them, and re-layouts  10 us
    all_gather x1, blocking collectives, shards(): key_row_tiles = lax.all_gather(picked, 'heads', axis=1, tiled=True)  8.8 us
    all_to_all x1, waiting for transfers between devices, shards(): lax.all_to_all(bundles, 'seq', split_axis=1, concat_axis=0, tiled=True)  7.21 us
    all_to_all x1, starting transfers between devices, shards(): lax.all_to_all(bundles, 'seq', split_axis=1, concat_axis=0, tiled=True)  5.51 us
    dot_general x1, matrix products, shards(): jnp.einsum('mfgv,mvq->mgfq', score_gradient, key_row_tiles, preferred_ele...  5.43 us
    dot_general x1, matrix products, shards(): jnp.einsum('bhtk,bkl->bthl', prob_half, value_rows, preferred_element_typ...  3.47 us
  transfers between devices with their start and end apart: 2, of which 2 were waited for; matrix products, arithmetic and copies ran while one was open for 7% of the time, Pallas kernels for 0%

commit v1 on v0

--- a/solution.py
+++ b/solution.py
@@ -52,7 +52,11 @@
         [key_gradient[:, :, :value_width] + grad_value, key_gradient[:, :, value_width:]], axis=-1
     )
     contrib = key_gradient.reshape(block_count * key_blocks, block_size, key_width)
-    head_total = lax.psum(contrib, "heads")
+    head_total = contrib
+    for hop in (1, 2):
+        head_total = head_total + lax.ppermute(
+            head_total, "heads", [(dev, dev ^ hop) for dev in range(4)]
+        )
     own_share = lax.dynamic_slice_in_dim(
         head_total, lax.axis_index("heads") * row_share, row_share, 1
     )

time: 151 us -> 142 us (0.940)
  between operations: 14.1 us -> 0.75 us
  waiting for transfers between devices: 51.3 us -> 44.5 us
  other arithmetic: 3.74 us -> 10.2 us
  local copies, waits for them, and re-layouts: 16.1 us -> 19.9 us
    psum x1 -> x0, waiting for transfers between devices: 44.1 us -> none  [shards(): head_total = lax.psum(contrib, 'heads')]
    ppermute x0 -> x2, waiting for transfers between devices: none -> 37.5 us  [shards(): lax.ppermute(head_total, 'heads', [(dev, dev ^ hop) for dev in range(4)])]
    add x0 -> x2, other arithmetic: none -> 6.44 us  [shards(): head_total + lax.ppermute(head_total, 'heads', [(dev, dev ^ hop) for dev...]
    reshape x0 -> x1, local copies, waits for them, and re-layouts: none -> 3.03 us  [shards(): key_gradient.reshape(block_count * key_blocks, block_size, key_width)]
  transfers between devices with their start and end apart: 2 -> 3, of which waited for: 2 -> 3; matrix products, arithmetic and copies ran while one was open for 7% -> 7% of each run, Pallas kernels for 0% -> 0%
where the time goes in v1:
time: 142 us; the launch traced here: 141 us
  waiting for transfers between devices  44.5 us (31%)
  blocking collectives  41.7 us (29%)
  local copies, waits for them, and re-layouts  19.9 us (14%)
  matrix products  17.9 us (13%)
  other arithmetic  10.2 us (7%)
  starting transfers between devices  6.41 us (5%)
    ppermute x2, waiting for transfers between devices, shards(): lax.ppermute(head_total, 'heads', [(dev, dev ^ hop) for dev in range(4)])  37.5 us
    all_gather x1, blocking collectives, shards(): slices = lax.all_gather(latents, 'seq', axis=0, tiled=True)  32.9 us
    unnamed x10, local copies, waits for them, and re-layouts  10 us
    all_gather x1, blocking collectives, shards(): key_row_tiles = lax.all_gather(picked, 'heads', axis=1, tiled=True)  8.8 us
    all_to_all x1, waiting for transfers between devices, shards(): lax.all_to_all(bundles, 'seq', split_axis=1, concat_axis=0, tiled=True)  7 us
    add x2, other arithmetic, shards(): head_total + lax.ppermute(head_total, 'heads', [(dev, dev ^ hop) for dev...  6.44 us
    all_to_all x1, starting transfers between devices, shards(): lax.all_to_all(bundles, 'seq', split_axis=1, concat_axis=0, tiled=True)  5.55 us
    dot_general x1, matrix products, shards(): jnp.einsum('mfgv,mvq->mgfq', score_gradient, key_row_tiles, preferred_ele...  5.43 us
  transfers between devices with their start and end apart: 3, of which 3 were waited for; matrix products, arithmetic and copies ran while one was open for 7% of the time, Pallas kernels for 0%

profile of v1, /device:TPU:0, one launch (start us, length us, event | category | flops | bytes accessed | tf_op | source)
XLA Modules:
  0.0 141.3 jit_solution(11885411975190001142)
XLA Ops:
  0.6 0.9 compare_and_fusion
  1.5 32.9 %all_gather.6 = bf16[8,32,576]{2,1,0:T(8,128)(2,1)S(1)} all-gather(bf16[1,32,576]{2,1,0:T(8,128)(2,1)} %param.5), channel_id=1, replica_groups=mesh['heads'=4,'seq'=8] {'seq'}, dimensions={0}, use_global_device_ids=true | all-gather | bytes 331776 | tf_op jit(solution)/shard_map/all_gather | solution.py:14
  34.4 0.6 gather_fusion
  35.0 0.1 broadcast_select_fusion
  35.1 8.8 %all_gather.7 = bf16[5,128,576]{2,1,0:T(8,128)(2,1)S(1)} all-gather(bf16[5,32,576]{2,1,0:T(8,128)(2,1)S(1)} %broadcast_select_fusion), channel_id=1, replica_groups=mesh['heads'=4,'seq'=8] {'heads'}, dimensions={1}, use_global_device_ids=true | all-gather | bytes 921600 | tf_op jit(solution)/shard_map/all_gather | solution.py:19
  43.9 4.8 %copy.56 = bf16[128,16,512]{0,2,1:T(8,128)(2,1)} copy(bf16[128,16,512]{2,1,0:T(8,128)(2,1)} %param.6) | data formatting | bytes 4194304 | tf_op args[2]
  48.7 2.2 %bitcast_reduce_fusion = (f32[16,128]{1,0:T(8,128)S(1)}, f32[640,128,16]{1,0,2:T(8,128)S(1)}) fusion(bf16[640,576,1]{1,0,2:T(8,128)(2,1)S(1)} %bitcast.124, bf16[128,16,576]{0,2,1:T(8,128)(2,1)S(1)} %copy-done), kind=kOutput, calls=%fused_computation.6 | convolution fusion | flops 1512568832 | bytes 8347648 | tf_op jit(solution)/shard_map/gonv,gmv->gnom/dot_general | solution.py:25
  50.9 0.9 fusion.5
  51.8 0.7 copy-done.1
  52.5 3.5 %fusion.6 = (f32[128,16]{0,1:T(8,128)S(1)}, bf16[512,16,128]{2,0,1:T(8,128)(2,1)}) fusion(bf16[128,16,512]{0,2,1:T(8,128)(2,1)S(1)} %copy-done.1, f32[16,128]{1,0:T(8,128)S(1)} %fusion.5, f32[16,128]{1,0:T(8,128)S(1)} %get-tuple-element.17, f32[640,128,16]{1,0,2:T(8,128)S(1)} %get-tuple-element.18, bf16[1,640,576]{2,1,0:T(8,128)(2,1)S(1)} %bitcast.125), kind=kOutput, calls=%fused_computation.11 | convolution fusion | flops 1352660992 | bytes 10117120 | tf_op jit(solution)/shard_map/bhtk,bkl->bthl/dot_general | solution.py:32
  56.0 2.2 %fusion.7 = bf16[16,128,640]{1,2,0:T(8,128)(2,1)S(1)} fusion(f32[16,128]{1,0:T(8,128)S(1)} %bitcast.130, f32[16,128]{1,0:T(8,128)S(1)} %fusion.5, f32[16,128]{1,0:T(8,128)S(1)} %get-tuple-element.17, f32[640,128,16]{1,0,2:T(8,128)S(1)} %get-tuple-element.18, bf16[128,16,512]{0,2,1:T(8,128)(2,1)S(1)} %copy-done.1, bf16[1,640,576]{2,1,0:T(8,128)(2,1)S(1)} %bitcast.126), kind=kOutput, calls=%fused_computation.12 | convolution fusion | flops 1351352320 | bytes 10641408 | tf_op jit(solution)/shard_map/bthl,bkl->bhtk/dot_general | solution.py:36
  58.2 2.0 %convolution_bitcast_fusion = f32[1,640,576]{1,2,0:T(8,128)S(1)} fusion(bf16[16,128,640]{1,2,0:T(8,128)(2,1)S(1)} %fusion.7, bf16[128,16,576]{0,2,1:T(8,128)(2,1)S(1)} %copy-done), kind=kOutput, calls=%fused_computation.22 | convolution fusion | flops 1509949440 | bytes 6455296 | tf_op jit(solution)/shard_map/jxnq,jnxa->jqa/dot_general | solution.py:45
  60.2 1.9 %fusion.19 = f32[1,640,512]{1,2,0:T(8,128)S(1)} fusion(bf16[128,16,512]{0,2,1:T(8,128)(2,1)S(1)} %copy-done.1, f32[1,640,576]{1,2,0:T(8,128)S(1)} %convolution_bitcast_fusion, f32[16,128]{1,0:T(8,128)S(1)} %fusion.5, f32[16,128]{1,0:T(8,128)S(1)} %get-tuple-element.17, f32[640,128,16]{1,0,2:T(8,128)S(1)} %get-tuple-element.18), kind=kOutput, calls=%fused_computation.24 | convolution fusion | flops 1347747840 | bytes 9977856 | tf_op jit(solution)/shard_map/bhtk,bthl->bkl/dot_general | solution.py:48
  62.2 1.2 pad_maximum_fusion
  63.4 3.0 %copy.62 = f32[1,640,576]{2,1,0:T(8,128)} copy(f32[1,640,576]{1,2,0:T(8,128)} %pad_maximum_fusion) | data formatting | bytes 2949120 | tf_op jit(solution)/shard_map/concatenate | solution.py:51
  66.4 3.0 %copy.64 = f32[5,128,576]{1,2,0:T(8,128)} copy(f32[5,128,576]{2,1,0:T(8,128)} %bitcast.121) | data formatting | bytes 2949120 | tf_op jit(solution)/shard_map/reshape | solution.py:54
  69.4 0.3 collective-permute-start
  69.8 3.1 %collective-permute-done = f32[5,128,576]{1,2,0:T(8,128)S(1)} collective-permute-done((f32[5,128,576]{1,2,0:T(8,128)}, f32[5,128,576]{1,2,0:T(8,128)S(1)}, u32[]{:S(2)}, u32[]{:S(2)}) %collective-permute-start) | collective-permute-done | bytes 1474592 | tf_op jit(solution)/shard_map/ppermute | solution.py:57
  72.9 2.7 %add.30 = f32[5,128,576]{1,2,0:T(8,128)} add(f32[5,128,576]{1,2,0:T(8,128)} %copy.64, f32[5,128,576]{1,2,0:T(8,128)S(1)} %collective-permute-done) | non-fusion elementwise | flops 368640 | bytes 4423680 | tf_op jit(solution)/shard_map/add | solution.py:57
  75.6 0.5 collective-permute-start.1
  76.1 34.4 %collective-permute-done.1 = f32[5,128,576]{1,2,0:T(8,128)} collective-permute-done((f32[5,128,576]{1,2,0:T(8,128)}, f32[5,128,576]{1,2,0:T(8,128)}, u32[]{:S(2)}, u32[]{:S(2)}) %collective-permute-start.1) | collective-permute-done | bytes 1474592 | tf_op jit(solution)/shard_map/ppermute | solution.py:57
  110.5 3.7 %dynamic-slice_add_fusion = f32[5,32,576]{1,2,0:T(8,128)} fusion(f32[5,128,576]{1,2,0:T(8,128)} %collective-permute-done.1, s32[]{:T(128)S(6)} %select_n.26, f32[5,128,576]{1,2,0:T(8,128)} %add.30), kind=kLoop, calls=%fused_computation.20 | loop fusion | flops 92160 | bytes 1105924 | tf_op jit(solution)/shard_map/add | solution.py:57
  114.2 1.8 %copy.65 = f32[5,32,576]{2,1,0:T(8,128)S(1)} copy(f32[5,32,576]{1,2,0:T(8,128)} %dynamic-slice_add_fusion) | data formatting | bytes 737280 | tf_op jit(solution)/shard_map/dynamic_slice | solution.py:60
  116.0 0.2 reshape.186
  116.3 0.2 dot_general.43
  116.5 0.7 convolution_bitcast_fusion.1
  117.1 1.0 copy.67
  118.1 5.6 %all-to-all-start = ((f32[1,8,32,576]{3,2,0,1:T(8,128)}), f32[1,8,32,576]{3,2,0,1:T(8,128)S(1)}, u32[]{:S(2)}, u32[]{:S(2)}) async-start(f32[1,8,32,576]{3,2,0,1:T(8,128)} %copy.67), calls=%async_computation | async-start | bytes 1310720 | tf_op jit(solution)/shard_map/all_to_all | solution.py:75
  123.7 4.5 %copy.68 = bf16[128,16,512]{2,1,0:T(8,128)(2,1)} copy(bf16[128,16,512]{0,2,1:T(8,128)(2,1)} %bitcast.123) | data formatting | bytes 4194304
  128.2 5.4 %convert_bitcast_fusion = bf16[128,16,576]{0,2,1:T(8,128)(2,1)} fusion(bf16[640,576,1]{1,0,2:T(8,128)(2,1)} %bitcast.127, bf16[16,128,640]{1,2,0:T(8,128)(2,1)} %copy-done.3), kind=kOutput, calls=%fused_computation.18 | convolution fusion | flops 1511129088 | bytes 5718016 | tf_op jit(solution)/shard_map/mfgv,mvq->mgfq/dot_general | solution.py:42
  133.6 7.0 %all-to-all-done = f32[1,8,32,576]{3,2,0,1:T(8,128)S(1)} async-done(((f32[1,8,32,576]{3,2,0,1:T(8,128)}), f32[1,8,32,576]{3,2,0,1:T(8,128)S(1)}, u32[]{:S(2)}, u32[]{:S(2)}) %all-to-all-start) | async-done | bytes 589856 | tf_op jit(solution)/shard_map/all_to_all | solution.py:75
  140.6 0.7 reduce_sum.34
  (10 shorter events, 0.0 us)
Async XLA Ops:
  0.6 48.1 %copy-start = (bf16[128,16,576]{0,2,1:T(8,128)(2,1)S(1)}, bf16[128,16,576]{0,2,1:T(8,128)(2,1)}, u32[]{:S(2)}) copy-start(bf16[128,16,576]{0,2,1:T(8,128)(2,1)} %param.4) | copy-start | bytes 7077892
  43.9 12.1 %copy-start.2 = (bf16[5,128,576]{2,1,0:T(8,128)(2,1)}, bf16[5,128,576]{2,1,0:T(8,128)(2,1)S(1)}, u32[]{:S(2)}) copy-start(bf16[5,128,576]{2,1,0:T(8,128)(2,1)S(1)} %all_gather.7) | copy-start | bytes 2211844
  50.9 1.6 %copy-start.1 = (bf16[128,16,512]{0,2,1:T(8,128)(2,1)S(1)}, bf16[128,16,512]{0,2,1:T(8,128)(2,1)}, u32[]{:S(2)}) copy-start(bf16[128,16,512]{0,2,1:T(8,128)(2,1)} %copy.56) | copy-start | bytes 6291460
  58.2 2.0 %copy-start.3 = (bf16[16,128,640]{1,2,0:T(8,128)(2,1)}, bf16[16,128,640]{1,2,0:T(8,128)(2,1)S(1)}, u32[]{:S(2)}) copy-start(bf16[16,128,640]{1,2,0:T(8,128)(2,1)S(1)} %fusion.7) | copy-start | bytes 7864324
  69.4 3.5 %collective-permute-start = (f32[5,128,576]{1,2,0:T(8,128)}, f32[5,128,576]{1,2,0:T(8,128)S(1)}, u32[]{:S(2)}, u32[]{:S(2)}) collective-permute-start(f32[5,128,576]{1,2,0:T(8,128)} %copy.64), channel_id=1, source_target_pairs={{0,8},{8,0},{16,24},{24,16},{1,9},{9,1},{17,25},{25,17},{2,10},{10... | collective-permute-start | bytes 4423688 | tf_op jit(solution)/shard_map/ppermute | solution.py:57
  75.6 34.9 %collective-permute-start.1 = (f32[5,128,576]{1,2,0:T(8,128)}, f32[5,128,576]{1,2,0:T(8,128)}, u32[]{:S(2)}, u32[]{:S(2)}) collective-permute-start(f32[5,128,576]{1,2,0:T(8,128)} %add.30), channel_id=1, source_target_pairs={{0,16},{8,24},{16,0},{24,8},{1,17},{9,25},{17,1},{25,9},{2,18},{10... | collective-permute-start | bytes 4423688 | tf_op jit(solution)/shard_map/ppermute | solution.py:57
  118.1 22.5 %all-to-all-start = ((f32[1,8,32,576]{3,2,0,1:T(8,128)}), f32[1,8,32,576]{3,2,0,1:T(8,128)S(1)}, u32[]{:S(2)}, u32[]{:S(2)}) async-start(f32[1,8,32,576]{3,2,0,1:T(8,128)} %copy.67), calls=%async_computation | async-start | bytes 1310720 | tf_op jit(solution)/shard_map/all_to_all | solution.py:75
